TPU v7x, 32 devices: a whole 2x2x4 slice. The times are simulated.
32 devices in a mesh: neur: 4 (over z), tri: 4 (over y, x), bin: 2 (over core).
Axes of the slice: x: 2, y: 2, z: 4, core: 2. Of those that a mesh axis runs over, the one named last changes fastest.
Arguments:
- tensor: bfloat16 [2048, 128, 256], P('neur', 'tri', 'bin'), may hold values from -3600 to 3600
- bin_factor: bfloat16 [256, 64], P('bin'), may hold values from 0.049804688 to 1
- trial_factor: bfloat16 [128, 64], P('tri'), may hold values from 0.049804688 to 1
Outputs:
- neuron_factor: float32 [2048, 64], P(('neur', 'tri', 'bin'))
- weights: float32 [64], replicated
All inputs are finite; a program needn't handle non-finite values.
Results may differ from a plain program's by a relative error of at most 0.0003.
Values sent between devices are 32-bit elements; how exact they have to be, the bound alone decides.
No kernel may reach another device: no remote copies, remote signals or barrier semaphores. Data moves between devices by JAX's collectives and lax.ppermute only.
A program may use at most 64 MiB of HBM per device.

v0:
```python
import jax
import jax.numpy as jnp
from jax import lax
from jax.sharding import PartitionSpec as P


def solve_rows(products, lower):
    return jax.scipy.linalg.cho_solve((lower, True), products.T).T


def local(tensor, bin_factor, trial_factor):
    rows, trials, bins = tensor.shape
    rank = bin_factor.shape[1]
    bin_part = jnp.dot(bin_factor.T, bin_factor, preferred_element_type=jnp.float32)
    trial_part = jnp.dot(trial_factor.T, trial_factor, preferred_element_type=jnp.float32)
    bin_gram = lax.psum(bin_part, "bin")
    trial_gram = lax.psum(trial_part, "tri")
    lower = jnp.linalg.cholesky(bin_gram * trial_gram)
    section = jnp.dot(
        tensor.reshape(rows * trials, bins), bin_factor, preferred_element_type=jnp.float32
    )
    section = section.reshape(rows, trials, rank)
    partial_value = jnp.sum(section * trial_factor.astype(jnp.float32)[None], axis=1)
    neurons_all = rows * lax.axis_size("neur")
    block = lax.psum(partial_value, ("tri", "bin"))
    block_solved = solve_rows(block, lower)
    squares = lax.psum(jnp.sum(block_solved * block_solved, axis=0), "neur")
    share = rows // (lax.axis_size("tri") * lax.axis_size("bin"))
    offset = (lax.axis_index("tri") * lax.axis_size("bin") + lax.axis_index("bin")) * share
    solved = lax.dynamic_slice_in_dim(block_solved, offset, share, 0)
    weights = jnp.sqrt(squares / neurons_all + 1e-06)
    return (solved / weights, weights)


def solution(mesh):
    return jax.shard_map(
        local,
        mesh=mesh,
        in_specs=(P("neur", "tri", "bin"), P("bin", None), P("tri", None)),
        out_specs=(P(("neur", "tri", "bin"), None), P()),
        check_vma=False,
    )
```

profile of v0, /device:TPU:0, one launch (start us, length us, event | category | flops | bytes accessed | tf_op | source)
XLA Modules:
  0.0 92.7 jit_solution(17252243305932020055)
XLA Ops:
  7.2 0.0 copy-start
  7.2 0.0 copy-start.1
  7.2 0.0 all-reduce.2.cloned.1.call-start
  7.2 0.7 convert_element_type.3
  8.0 0.0 copy-done
  8.0 7.6 %multiply_reduce_fusion = f32[512,64]{0,1:T(8,128)} fusion(bf16[512,32,128]{2,1,0:T(8,128)(2,1)} %param.3, f32[32,64]{1,0:T(8,128)S(1)} %convert_element_type.3, bf16[128,64]{0,1:T(8,128)(2,1)S(1)} %copy-done), kind=kOutput, calls=%fused_computation.2 | convolution fusion | flops 270499840 | bytes 4349952 | tf_op jit(solution)/shard_map/dot_general | solution.py:19
  15.5 0.0 all-reduce.2.cloned.1.call-update
  15.5 0.1 fusion.11
  15.7 0.0 copy-done.1
  15.7 0.2 fusion.12
  15.9 3.7 %psum.28 = f32[64,64]{0,1:T(8,128)S(1)} all-reduce(f32[64,64]{0,1:T(8,128)S(1)} %fusion.11), channel_id=1, replica_groups=mesh['neur'=4,'tri'=4,'bin'=2] {'bin'}, use_global_device_ids=true, to_apply=%region_0.0 | all-reduce | flops 4096 | bytes 32768 | tf_op jit(solution)/shard_map/psum | solution.py:16
  19.6 17.5 %psum.29 = f32[64,64]{0,1:T(8,128)S(1)} all-reduce(f32[64,64]{0,1:T(8,128)S(1)} %fusion.12), channel_id=1, replica_groups=mesh['neur'=4,'tri'=4,'bin'=2] {'tri'}, use_global_device_ids=true, to_apply=%region_1.0 | all-reduce | flops 4096 | bytes 32768 | tf_op jit(solution)/shard_map/psum | solution.py:17
  37.1 0.1 copy.11
  37.1 5.9 %cholesky.16 = f32[64,64]{1,0:T(8,128)S(1)} custom-call(f32[64,64]{1,0:T(8,128)S(1)} %fusion.9), custom_call_target="Cholesky" | custom-call | tf_op jit(solution)/shard_map/jit(cholesky)/cholesky | solution.py:18
  43.0 0.6 compare_reduce_fusion
  43.7 0.7 fusion.4
  44.3 4.9 %custom-call.10 = f32[1,64,64]{1,2,0:T(8,128)S(1)} custom-call(f32[1,64,64]{2,1,0:T(8,128)S(1)} %fusion.4), custom_call_target="InvertDiagBlocksLowerTriangular" | custom-call | tf_op jit(solution)/shard_map/jit(_cho_solve)/triangular_solve | solution.py:8
  49.2 22.5 %all-reduce.2.cloned.1.call-done = f32[512,64]{0,1:T(8,128)} async-done(((f32[512,64]{0,1:T(8,128)}), f32[512,64]{0,1:T(8,128)}) %all-reduce.2.cloned.1.call-update) | async-done | bytes 131088 | tf_op jit(solution)/shard_map/psum | solution.py:25
  71.8 1.2 %fusion.7 = f32[64,512]{1,0:T(8,128)S(1)} fusion(f32[512,64]{0,1:T(8,128)} %all-reduce.2.cloned.1.call-done, f32[1,64,64]{1,2,0:T(8,128)S(1)} %custom-call.10), kind=kOutput, calls=%fused_computation.8 | convolution fusion | flops 25165824 | bytes 278528 | tf_op jit(solution)/shard_map/jit(_cho_solve)/triangular_solve | solution.py:8
  73.0 0.4 multiply_reduce_fusion.1
  73.4 11.7 %psum.31 = f32[64]{0:T(128)S(1)} all-reduce(f32[64]{0:T(128)S(1)} %get-tuple-element.6), channel_id=1, replica_groups=mesh['neur'=4,'tri'=4,'bin'=2] {'neur'}, use_global_device_ids=true, to_apply=%region_7.8 | all-reduce | flops 64 | bytes 512 | tf_op jit(solution)/shard_map/psum | solution.py:27
  85.1 0.0 copy-start.2
  85.1 0.1 dynamic-slice_divide_fusion
  85.2 0.7 copy.12
  85.9 0.0 copy-done.2
  (4 shorter events, 0.1 us)
Async XLA Ops:
  7.2 0.8 copy-start
  7.2 8.5 %copy-start.1 = (bf16[32,64]{1,0:T(8,128)(2,1)S(1)}, bf16[32,64]{1,0:T(8,128)(2,1)}, u32[]{:S(2)}) copy-start(bf16[32,64]{1,0:T(8,128)(2,1)} %param.5) | copy-start | bytes 12292
  7.2 64.6 %all-reduce.2.cloned.1.call-start = ((), (), s32[]{:S(2)}) async-start(), calls=%async_computation | async-start | bytes 262144 | tf_op jit(solution)/shard_map/psum | solution.py:25
  85.1 0.8 copy-start.2
Sparse Core Ops, SparseCore 0:
  15.7 56.0 all-reduce.1
where the time goes:
time: 93.1 us; the launch traced here: 92.7 us
  blocking collectives  32.8 us (35%)
  waiting for transfers between devices  22.6 us (24%)
  between operations  14.1 us (15%)
  other arithmetic  12.9 us (14%)
  matrix products  9.46 us (10%)
    psum x1, waiting for transfers between devices, local(): block = lax.psum(partial_value, ('tri', 'bin'))  22.5 us
    psum x1, blocking collectives, local(): trial_gram = lax.psum(trial_part, 'tri')  17.5 us
    psum x1, blocking collectives, local(): squares = lax.psum(jnp.sum(block_solved * block_solved, axis=0), 'neur')  11.7 us
    dot_general x1, matrix products, local(): jnp.dot(tensor.reshape(rows * trials, bins), bin_factor, preferred_elemen...  7.56 us
    another operation x3, other arithmetic, local(): lower = jnp.linalg.cholesky(bin_gram * trial_gram)  6.53 us
    another operation x2, other arithmetic, solve_rows(): return jax.scipy.linalg.cho_solve((lower, True), products.T).T  5.55 us
    psum x1, blocking collectives, local(): bin_gram = lax.psum(bin_part, 'bin')  3.68 us
  transfers between devices with their start and end apart: 1, of which 1 were waited for; matrix products, arithmetic and copies ran while one was open for 13% of the time, Pallas kernels for 0%

commit v1 on v0

--- a/solution.py
+++ b/solution.py
@@ -22,7 +22,7 @@
     section = section.reshape(rows, trials, rank)
     partial_value = jnp.sum(section * trial_factor.astype(jnp.float32)[None], axis=1)
     neurons_all = rows * lax.axis_size("neur")
-    block = lax.psum(partial_value, ("tri", "bin"))
+    block = lax.psum(lax.psum(partial_value, "bin"), "tri")
     block_solved = solve_rows(block, lower)
     squares = lax.psum(jnp.sum(block_solved * block_solved, axis=0), "neur")
     share = rows // (lax.axis_size("tri") * lax.axis_size("bin"))

time: 93.1 us -> 107 us (1.15)
  waiting for transfers between devices: 22.6 us -> 36.1 us
    psum x1 -> x2, waiting for transfers between devices: 22.5 us -> 36.1 us  [local(): block = lax.psum(lax.psum(partial_value, 'bin'), 'tri')]
  transfers between devices with their start and end apart: 1 -> 2, of which waited for: 1 -> 1; matrix products, arithmetic and copies ran while one was open for 13% -> 12% of each run, Pallas kernels for 0% -> 0%
where the time goes in v1:
time: 107 us; the launch traced here: 106 us
  waiting for transfers between devices  36.1 us (34%)
  blocking collectives  32.8 us (31%)
  between operations  14.1 us (13%)
  other arithmetic  12.9 us (12%)
  matrix products  9.47 us (9%)
    psum x2, waiting for transfers between devices, local(): block = lax.psum(lax.psum(partial_value, 'bin'), 'tri')  36.1 us
    psum x1, blocking collectives, local(): trial_gram = lax.psum(trial_part, 'tri')  17.5 us
    psum x1, blocking collectives, local(): squares = lax.psum(jnp.sum(block_solved * block_solved, axis=0), 'neur')  11.7 us
    dot_general x1, matrix products, local(): jnp.dot(tensor.reshape(rows * trials, bins), bin_factor, preferred_elemen...  7.56 us
    another operation x3, other arithmetic, local(): lower = jnp.linalg.cholesky(bin_gram * trial_gram)  6.52 us
    another operation x2, other arithmetic, solve_rows(): return jax.scipy.linalg.cho_solve((lower, True), products.T).T  5.55 us
    psum x1, blocking collectives, local(): bin_gram = lax.psum(bin_part, 'bin')  3.68 us
  transfers between devices with their start and end apart: 2, of which 1 were waited for; matrix products, arithmetic and copies ran while one was open for 12% of the time, Pallas kernels for 0%

profile of v1, /device:TPU:0, one launch (start us, length us, event | category | flops | bytes accessed | tf_op | source)
XLA Modules:
  0.0 106.3 jit_solution(16199475057268770363)
XLA Ops:
  7.2 0.0 copy-start
  7.2 0.0 copy-start.1
  7.2 0.0 all-reduce.3.cloned.1.call-start
  7.2 0.7 convert_element_type.3
  8.0 0.0 copy-done
  8.0 7.6 %multiply_reduce_fusion = f32[512,64]{0,1:T(8,128)} fusion(bf16[512,32,128]{2,1,0:T(8,128)(2,1)} %param.3, f32[32,64]{1,0:T(8,128)S(1)} %convert_element_type.3, bf16[128,64]{0,1:T(8,128)(2,1)S(1)} %copy-done), kind=kOutput, calls=%fused_computation.2 | convolution fusion | flops 270499840 | bytes 4349952 | tf_op jit(solution)/shard_map/dot_general | solution.py:19
  15.5 0.0 all-reduce.3.cloned.1.call-update
  15.5 0.0 all-reduce.5.cloned.1.call-start
  15.6 0.1 fusion.11
  15.7 0.0 copy-done.1
  15.7 0.2 fusion.12
  15.9 3.7 %psum.35 = f32[64,64]{0,1:T(8,128)S(1)} all-reduce(f32[64,64]{0,1:T(8,128)S(1)} %fusion.11), channel_id=1, replica_groups=mesh['neur'=4,'tri'=4,'bin'=2] {'bin'}, use_global_device_ids=true, to_apply=%region_0.0 | all-reduce | flops 4096 | bytes 32768 | tf_op jit(solution)/shard_map/psum | solution.py:16
  19.6 17.5 %psum.36 = f32[64,64]{0,1:T(8,128)S(1)} all-reduce(f32[64,64]{0,1:T(8,128)S(1)} %fusion.12), channel_id=1, replica_groups=mesh['neur'=4,'tri'=4,'bin'=2] {'tri'}, use_global_device_ids=true, to_apply=%region_1.0 | all-reduce | flops 4096 | bytes 32768 | tf_op jit(solution)/shard_map/psum | solution.py:17
  37.1 0.1 copy.11
  37.2 5.8 %cholesky.16 = f32[64,64]{1,0:T(8,128)S(1)} custom-call(f32[64,64]{1,0:T(8,128)S(1)} %fusion.9), custom_call_target="Cholesky" | custom-call | tf_op jit(solution)/shard_map/jit(cholesky)/cholesky | solution.py:18
  43.1 0.6 compare_reduce_fusion
  43.7 0.0 all-reduce.3.cloned.1.call-done
  43.7 0.0 all-reduce.5.cloned.1.call-update
  43.7 0.7 fusion.4
  44.4 4.9 %custom-call.10 = f32[1,64,64]{1,2,0:T(8,128)S(1)} custom-call(f32[1,64,64]{2,1,0:T(8,128)S(1)} %fusion.4), custom_call_target="InvertDiagBlocksLowerTriangular" | custom-call | tf_op jit(solution)/shard_map/jit(_cho_solve)/triangular_solve | solution.py:8
  49.3 36.1 %all-reduce.5.cloned.1.call-done = f32[512,64]{0,1:T(8,128)} async-done(((f32[512,64]{0,1:T(8,128)}), f32[512,64]{0,1:T(8,128)}) %all-reduce.5.cloned.1.call-update) | async-done | bytes 131088 | tf_op jit(solution)/shard_map/psum | solution.py:25
  85.4 1.2 %fusion.7 = f32[64,512]{1,0:T(8,128)S(1)} fusion(f32[512,64]{0,1:T(8,128)} %all-reduce.5.cloned.1.call-done, f32[1,64,64]{1,2,0:T(8,128)S(1)} %custom-call.10), kind=kOutput, calls=%fused_computation.8 | convolution fusion | flops 25165824 | bytes 278528 | tf_op jit(solution)/shard_map/jit(_cho_solve)/triangular_solve | solution.py:8
  86.6 0.4 multiply_reduce_fusion.1
  87.0 11.7 %psum.39 = f32[64]{0:T(128)S(1)} all-reduce(f32[64]{0:T(128)S(1)} %get-tuple-element.6), channel_id=1, replica_groups=mesh['neur'=4,'tri'=4,'bin'=2] {'neur'}, use_global_device_ids=true, to_apply=%region_8.9 | all-reduce | flops 64 | bytes 512 | tf_op jit(solution)/shard_map/psum | solution.py:27
  98.7 0.0 copy-start.2
  98.7 0.1 dynamic-slice_divide_fusion
  98.8 0.7 copy.12
  99.5 0.0 copy-done.2
  (4 shorter events, 0.1 us)
Async XLA Ops:
  7.2 0.8 copy-start
  7.2 8.5 %copy-start.1 = (bf16[32,64]{1,0:T(8,128)(2,1)S(1)}, bf16[32,64]{1,0:T(8,128)(2,1)}, u32[]{:S(2)}) copy-start(bf16[32,64]{1,0:T(8,128)(2,1)} %param.5) | copy-start | bytes 12292
  7.2 36.5 %all-reduce.3.cloned.1.call-start = ((), (), s32[]{:S(2)}) async-start(), calls=%async_computation | async-start | bytes 262144 | tf_op jit(solution)/shard_map/psum | solution.py:25
  15.5 69.8 %all-reduce.5.cloned.1.call-start = ((), (), s32[]{:S(2)}) async-start(), calls=%async_computation.1 | async-start | bytes 262144 | tf_op jit(solution)/shard_map/psum | solution.py:25
  98.7 0.8 copy-start.2
Sparse Core Ops, SparseCore 0:
  15.7 20.6 all-reduce.2
  43.9 41.4 all-reduce.4
